TPU v7x, 256 devices: a whole 4x4x8 slice. The times are simulated.
256 devices in a mesh: sub: 128 (over x_lo, y, z, core), row: 2 (over x_hi).
Axes of the slice: x: 4 (x_hi: 2, x_lo: 2; x = x_hi * 2 + x_lo), y: 4, z: 8, core: 2. Of those that a mesh axis runs over, the one named last changes fastest.
Arguments:
- compliance: bfloat16 [128, 36, 18, 128, 128], P('sub', 'row'), may hold values from -0.0625 to 0.0625
- block_columns: int32 [128, 36, 18], P('sub', 'row'), may hold values from 0 to 35, as said below
- load_response: bfloat16 [128, 32, 4608], P('sub', None, 'row'), may hold values from -6 to 6
- starting_motion: bfloat16 [128, 32, 4608], P('sub', None, 'row'), may hold values from -6 to 6
- start_traction: bfloat16 [128, 32, 4608], P('sub', None, 'row'), may hold values from -6 to 6
- stiffness: float32 [128, 4608], P('sub', 'row'), may hold values from 1 to 10
- history: float32 [128, 4608], P('sub', 'row'), may hold values from 0 to 0.6
- face_partner: int32 [128, 36], P('sub', 'row'), may hold values from -1 to 8, as said below
- orientation: int32 [128, 36, 128], P('sub', 'row'), may hold values from 0 to 127, as said below
Outputs:
- displacement: bfloat16 [128, 32, 4608], P('sub', None, 'row')
- traction: bfloat16 [128, 32, 4608], P('sub', None, 'row')
Inputs may be any that keep to these rules, and one draw needn't show every extreme that they name: `block_columns`: each block row names 18 distinct face columns. `face_partner`: an entry is -1 for a free face, else the position, within the facing group of the same run of the neighbouring substructure, of the matched face. Matches are mutual. Faces facing s+1 on the last substructure and faces facing s-1 on the first are free. In some run of some substructure all 9 faces facing s+1 are matched. `orientation`: each face's row is a permutation of 0 to 127; matched faces carry mutually inverse permutations.
All inputs are finite; a program needn't handle non-finite values.
Results may differ from a plain program's by a relative error of at most 0.0045.
The roundings to bfloat16 on the way count: a program that leaves them out, or rounds other values in their place, can miss the bound.
Values may be sent and summed in bfloat16 or wider, within the bound.
A program may use at most 64 MiB of HBM per device.

v0:
```python
import jax
import jax.numpy as jnp
from jax import lax
from jax.sharding import PartitionSpec as P

SURFACE_EXTENT = 128
ITERS = 3


search_stiffness = 1.0
onset_jump = 0.15
failure_jump = 1.5


def with_halo(cells, sides, width):
    for axis, dim in sides:
        count = lax.axis_size(axis)
        ends = count - 1
        head = lax.slice_in_dim(cells, 0, width, axis=dim)
        tail = lax.slice_in_dim(cells, cells.shape[dim] - width, cells.shape[dim], axis=dim)
        cells = jnp.concatenate(
            [
                lax.ppermute(tail, axis, [(i, (i + 1) % count) for i in range(ends)]),
                cells,
                lax.ppermute(head, axis, [((i + 1) % count, i) for i in range(ends)]),
            ],
            axis=dim,
        )
    return cells


def cohesive(upward_marker, constitutive_parameters, opposing_surface, live_mask):
    temporal_points = upward_marker.shape[0]
    mate_upward_marker = opposing_surface[:temporal_points]
    joint_rigidity = 0.5 * (constitutive_parameters[0] + opposing_surface[temporal_points])
    joint_record = jnp.maximum(constitutive_parameters[1], opposing_surface[temporal_points + 1])
    difference = upward_marker - mate_upward_marker
    jump_size = difference / (search_stiffness + 2.0 * joint_rigidity)
    running_peak = lax.associative_scan(jnp.maximum, jnp.abs(jump_size), axis=0)
    peak_jump = jnp.maximum(joint_record, running_peak)
    damage = jnp.clip((peak_jump - onset_jump) / (failure_jump - onset_jump), 0.0, 1.0)
    effective = joint_rigidity * (1.0 - damage)
    traction = jnp.where(
        live_mask, effective * difference / (search_stiffness + 2.0 * effective), 0.0
    )
    displacement = (traction - upward_marker) / search_stiffness
    return (displacement, traction)


def shards(
    compliance,
    block_columns,
    load_response,
    starting_motion,
    start_traction,
    stiffness,
    history,
    face_partner,
    orientation,
):
    compliance_rows = compliance[0]
    columns = block_columns[0]
    temporal_points = starting_motion.shape[1]
    segment_breadth = starting_motion.shape[2]
    number_surfaces = segment_breadth // SURFACE_EXTENT
    group_size = number_surfaces // 2
    stored_blocks = columns.shape[1]
    applied_forces = load_response[0].astype(jnp.float32)
    constitutive_parameters = jnp.stack([stiffness[0], history[0]]).reshape(
        2, number_surfaces, SURFACE_EXTENT
    )
    partner_table = face_partner[0]
    turning = orientation[0]
    turn_table = (
        turning[:, :, None] == jnp.arange(SURFACE_EXTENT, dtype=jnp.int32)[None, None, :]
    ).astype(jnp.float32)
    facing_up = jnp.arange(number_surfaces) < group_size
    live_mask = (partner_table >= 0)[:, None]
    safe_index = jnp.maximum(partner_table, 0)
    source = jnp.where(facing_up, safe_index, group_size + safe_index)
    present_motion = starting_motion[0].astype(jnp.float32)
    present_stress = start_traction[0].astype(jnp.float32)
    for iteration in range(ITERS):
        robin_sum = present_stress + search_stiffness * present_motion
        gathered_entries = lax.all_gather(robin_sum.astype(jnp.bfloat16), "row", axis=1, tiled=True)
        flexibility_tiles = gathered_entries.reshape(temporal_points, -1, SURFACE_EXTENT)

        def add_block(index, total):
            column_slice = lax.dynamic_index_in_dim(columns, index, 1, keepdims=False)
            piece = jnp.take(flexibility_tiles, column_slice, axis=1)
            block = lax.dynamic_index_in_dim(compliance_rows, index, 1, keepdims=False)
            return total + jnp.einsum(
                "tib,iab->tia", piece, block, preferred_element_type=jnp.float32
            )

        starting_total = jnp.zeros((temporal_points, number_surfaces, SURFACE_EXTENT), jnp.float32)
        operator_multiply = lax.fori_loop(0, stored_blocks, add_block, starting_total)
        proportional_reaction = (
            operator_multiply.reshape(temporal_points, segment_breadth) + applied_forces
        )
        upward_marker = (robin_sum - 2.0 * search_stiffness * proportional_reaction).reshape(
            temporal_points, number_surfaces, SURFACE_EXTENT
        )
        payload = jnp.concatenate([upward_marker, constitutive_parameters], axis=0)[None]
        neighbours = with_halo(payload, (("sub", 0),), 1)
        below_faces = neighbours[0, :, :group_size]
        above_faces = neighbours[2, :, group_size:]
        combined = jnp.concatenate([above_faces, below_faces], axis=1)
        chosen = jnp.take(combined, source, axis=1)
        opposing_surface = jnp.einsum(
            "tfy,fxy->tfx", chosen, turn_table, precision=lax.Precision.HIGHEST
        )
        motion_distribution, stress_distribution = cohesive(
            upward_marker, constitutive_parameters, opposing_surface, live_mask
        )
        present_motion = motion_distribution.reshape(temporal_points, segment_breadth)
        present_stress = stress_distribution.reshape(temporal_points, segment_breadth)
    return (present_motion.astype(jnp.bfloat16)[None], present_stress.astype(jnp.bfloat16)[None])


def solution(mesh):
    in_specs = (
        P("sub", "row", None, None, None),
        P("sub", "row", None),
        P("sub", None, "row"),
        P("sub", None, "row"),
        P("sub", None, "row"),
        P("sub", "row"),
        P("sub", "row"),
        P("sub", "row"),
        P("sub", "row", None),
    )
    out_specs = (P("sub", None, "row"), P("sub", None, "row"))
    return jax.shard_map(shards, mesh=mesh, in_specs=in_specs, out_specs=out_specs, check_vma=False)
```

profile of v0, /device:TPU:2, one launch (start us, length us, event | category | flops | bytes accessed | tf_op | source)
XLA Modules:
  0.0 213.1 jit_solution(7037482593136003585)
XLA Ops:
  1.7 9.7 %copy.62 = bf16[1,18,18,128,128]{4,3,1,2,0:T(8,128)(2,1)} copy(bf16[1,18,18,128,128]{4,3,2,1,0:T(8,128)(2,1)} %param.19) | data formatting | bytes 21233664 | tf_op args[0]
  11.5 7.7 %all-gather = bf16[1,32,4608]{2,1,0:T(8,128)(2,1)S(1)} all-gather(bf16[1,32,2304]{2,1,0:T(8,128)(2,1)S(1)} %get-tuple-element.411), channel_id=2, replica_groups=mesh['sub'=128,'row'=2] {'row'}, dimensions={2}, use_global_device_ids=true | all-gather | bytes 442368 | tf_op jit(solution)/shard_map/all_gather | solution.py:85
  19.5 38.6 %while.42 = (s32[]{:T(128)}, f32[32,18,128]{2,0,1:T(8,128)S(1)}, bf16[18,18,128,128]{3,2,0,1:T(8,128)(2,1)}, s32[18,18]{0,1:T(8,128)S(1)}, bf16[32,36,128]{2,0,1:T(8,128)(2,1)S(1)}, /*index=5*/s32[]{:T(128)}, s32[]{:T(128)}) while((s32[]{:T(128)}, f32[32,18,128]{2,0,1:T(8,128)S(1)}, bf16[18,18,128,128]{3,2,0,1:T(8,128)(2,1)}, ...), condition=%wide.region_1.0_spmd.clone, body=%wide.region_0.2_spmd.clone.sunk | while | flops 19096688 | bytes 1626539 | solution.py:97
  20.1 1.5 fusion.72
  22.3 1.5 fusion.72
  24.4 1.5 fusion.72
  26.6 1.5 fusion.72
  28.7 1.5 fusion.72
  30.9 1.5 fusion.72
  33.0 1.5 fusion.72
  35.2 1.5 fusion.72
  58.5 1.9 collective-permute-start.1
  60.4 8.8 %collective-permute-start = (f32[1,34,18,128]{3,1,2,0:T(8,128)S(1)}, f32[1,34,18,128]{3,1,2,0:T(8,128)S(1)}, u32[]{:S(2)}, u32[]{:S(2)}) collective-permute-start(f32[1,34,18,128]{3,1,2,0:T(8,128)S(1)} %fusion.30), channel_id=1, source_target_pairs={{2,0},{4,2},{6,4},{8,6},{10,8},{12,10},{14,12},{16,14},{18,16},{20... | collective-permute-start | bytes 940040 | tf_op jit(solution)/shard_map/ppermute | solution.py:25
  69.3 3.2 %collective-permute-done.1 = f32[1,34,18,128]{3,1,2,0:T(8,128)S(1)} collective-permute-done((f32[1,34,18,128]{3,1,2,0:T(8,128)S(1)}, f32[1,34,18,128]{3,1,2,0:T(8,128)S(1)}, u32[]{:S(2)}, u32[]{:S(2)}) %collective-permute-start.1) | collective-permute-done | bytes 313376 | tf_op jit(solution)/shard_map/ppermute | solution.py:23
  72.5 1.7 collective-permute-done
  74.8 1.7 convolution_bitcast_fusion.5
  79.3 7.3 %all_gather.10 = bf16[32,4608]{1,0:T(8,128)(2,1)S(1)} all-gather(bf16[32,2304]{1,0:T(8,128)(2,1)S(1)} %bitcast.172), channel_id=1, replica_groups=mesh['sub'=128,'row'=2] {'row'}, dimensions={1}, use_global_device_ids=true | all-gather | bytes 442368 | tf_op jit(solution)/shard_map/all_gather | solution.py:85
  86.7 38.6 %while.43 = (s32[]{:T(128)}, f32[32,18,128]{2,0,1:T(8,128)S(1)}, bf16[18,18,128,128]{3,2,0,1:T(8,128)(2,1)}, s32[18,18]{0,1:T(8,128)S(1)}, bf16[32,36,128]{2,0,1:T(8,128)(2,1)S(1)}, /*index=5*/s32[]{:T(128)}, s32[]{:T(128)}) while((s32[]{:T(128)}, f32[32,18,128]{2,0,1:T(8,128)S(1)}, bf16[18,18,128,128]{3,2,0,1:T(8,128)(2,1)}, ...), condition=%wide.region_3.6_spmd.clone, body=%wide.region_2.5_spmd.clone.sunk | while | flops 19096688 | bytes 1626539 | solution.py:97
  117.3 1.5 fusion.75
  125.5 1.9 collective-permute-start.3
  127.4 7.9 %collective-permute-start.2 = (f32[1,34,18,128]{3,1,2,0:T(8,128)S(1)}, f32[1,34,18,128]{3,1,2,0:T(8,128)S(1)}, u32[]{:S(2)}, u32[]{:S(2)}) collective-permute-start(f32[1,34,18,128]{3,1,2,0:T(8,128)S(1)} %fusion.31), channel_id=1, source_target_pairs={{2,0},{4,2},{6,4},{8,6},{10,8},{12,10},{14,12},{16,14},{18,16},{20... | collective-permute-start | bytes 940040 | tf_op jit(solution)/shard_map/ppermute | solution.py:25
  135.3 3.2 %collective-permute-done.3 = f32[1,34,18,128]{3,1,2,0:T(8,128)S(1)} collective-permute-done((f32[1,34,18,128]{3,1,2,0:T(8,128)S(1)}, f32[1,34,18,128]{3,1,2,0:T(8,128)S(1)}, u32[]{:S(2)}, u32[]{:S(2)}) %collective-permute-start.3) | collective-permute-done | bytes 313376 | tf_op jit(solution)/shard_map/ppermute | solution.py:23
  138.5 1.7 collective-permute-done.2
  140.9 1.7 convolution_bitcast_fusion.4
  145.4 7.3 %all_gather.11 = bf16[32,4608]{1,0:T(8,128)(2,1)S(1)} all-gather(bf16[32,2304]{1,0:T(8,128)(2,1)S(1)} %bitcast.173), channel_id=1, replica_groups=mesh['sub'=128,'row'=2] {'row'}, dimensions={1}, use_global_device_ids=true | all-gather | bytes 442368 | tf_op jit(solution)/shard_map/all_gather | solution.py:85
  152.7 38.6 %while.44 = (s32[]{:T(128)}, f32[32,18,128]{2,0,1:T(8,128)S(1)}, bf16[18,18,128,128]{3,2,0,1:T(8,128)(2,1)}, s32[18,18]{0,1:T(8,128)S(1)}, bf16[32,36,128]{2,0,1:T(8,128)(2,1)S(1)}, /*index=5*/s32[]{:T(128)}, s32[]{:T(128)}) while((s32[]{:T(128)}, f32[32,18,128]{2,0,1:T(8,128)S(1)}, bf16[18,18,128,128]{3,2,0,1:T(8,128)(2,1)}, ...), condition=%wide.region_5.8_spmd.clone, body=%wide.region_4.7_spmd.clone.sunk | while | flops 19096688 | bytes 1626539 | solution.py:97
  172.7 1.5 fusion.78
  191.5 1.9 collective-permute-start.5
  193.5 7.9 %collective-permute-start.4 = (f32[1,34,18,128]{3,1,2,0:T(8,128)S(1)}, f32[1,34,18,128]{3,1,2,0:T(8,128)S(1)}, u32[]{:S(2)}, u32[]{:S(2)}) collective-permute-start(f32[1,34,18,128]{3,1,2,0:T(8,128)S(1)} %fusion.32), channel_id=1, source_target_pairs={{2,0},{4,2},{6,4},{8,6},{10,8},{12,10},{14,12},{16,14},{18,16},{20... | collective-permute-start | bytes 940040 | tf_op jit(solution)/shard_map/ppermute | solution.py:25
  201.3 3.3 %collective-permute-done.5 = f32[1,34,18,128]{3,1,2,0:T(8,128)S(1)} collective-permute-done((f32[1,34,18,128]{3,1,2,0:T(8,128)S(1)}, f32[1,34,18,128]{3,1,2,0:T(8,128)S(1)}, u32[]{:S(2)}, u32[]{:S(2)}) %collective-permute-start.5) | collective-permute-done | bytes 313376 | tf_op jit(solution)/shard_map/ppermute | solution.py:23
  204.6 1.7 collective-permute-done.4
  207.0 1.7 convolution_bitcast_fusion.3
  (393 shorter events, 112.0 us)
Async XLA Ops:
  1.7 9.7 %copy-start.3 = (s32[1,18,18]{2,0,1:T(1,128)S(1)}, s32[1,18,18]{2,0,1:T(1,128)}, u32[]{:S(2)}) copy-start(s32[1,18,18]{2,0,1:T(1,128)} %param.20) | copy-start | bytes 3892
  1.7 56.4 %copy-start = (bf16[1,32,2304]{2,1,0:T(8,128)(2,1)S(1)}, bf16[1,32,2304]{2,1,0:T(8,128)(2,1)}, u32[]{:S(2)}) copy-start(bf16[1,32,2304]{2,1,0:T(8,128)(2,1)} %param.21) | copy-start | bytes 442372
  11.4 46.8 %copy-start.1 = (f32[1,2304]{1,0:T(1,128)S(1)}, f32[1,2304]{1,0:T(1,128)}, u32[]{:S(2)}) copy-start(f32[1,2304]{1,0:T(1,128)} %param.25) | copy-start | bytes 27652
  11.4 46.9 %copy-start.2 = (f32[1,2304]{1,0:T(1,128)S(1)}, f32[1,2304]{1,0:T(1,128)}, u32[]{:S(2)}) copy-start(f32[1,2304]{1,0:T(1,128)} %param.24) | copy-start | bytes 27652
  11.4 57.8 %copy-start.4 = (s32[1,18,128]{2,0,1:T(1,128)S(1)}, s32[1,18,128]{2,0,1:T(1,128)}, u32[]{:S(2)}) copy-start(s32[1,18,128]{2,0,1:T(1,128)} %param.27) | copy-start | bytes 27652
  11.4 57.8 %copy-start.5 = (s32[1,18]{1,0:T(1,128)S(1)}, s32[1,18]{1,0:T(1,128)}, u32[]{:S(2)}) copy-start(s32[1,18]{1,0:T(1,128)} %param.26) | copy-start | bytes 220
  58.5 14.0 %collective-permute-start.1 = (f32[1,34,18,128]{3,1,2,0:T(8,128)S(1)}, f32[1,34,18,128]{3,1,2,0:T(8,128)S(1)}, u32[]{:S(2)}, u32[]{:S(2)}) collective-permute-start(f32[1,34,18,128]{3,1,2,0:T(8,128)S(1)} %fusion.30), channel_id=1, source_target_pairs={{0,2},{2,4},{4,6},{6,8},{8,10},{10,12},{12,14},{14,16},{16,18},{18... | collective-permute-start | bytes 940040 | tf_op jit(solution)/shard_map/ppermute | solution.py:23
  60.4 13.8 %collective-permute-start = (f32[1,34,18,128]{3,1,2,0:T(8,128)S(1)}, f32[1,34,18,128]{3,1,2,0:T(8,128)S(1)}, u32[]{:S(2)}, u32[]{:S(2)}) collective-permute-start(f32[1,34,18,128]{3,1,2,0:T(8,128)S(1)} %fusion.30), channel_id=1, source_target_pairs={{2,0},{4,2},{6,4},{8,6},{10,8},{12,10},{14,12},{16,14},{18,16},{20... | collective-permute-start | bytes 940040 | tf_op jit(solution)/shard_map/ppermute | solution.py:25
  125.5 13.1 %collective-permute-start.3 = (f32[1,34,18,128]{3,1,2,0:T(8,128)S(1)}, f32[1,34,18,128]{3,1,2,0:T(8,128)S(1)}, u32[]{:S(2)}, u32[]{:S(2)}) collective-permute-start(f32[1,34,18,128]{3,1,2,0:T(8,128)S(1)} %fusion.31), channel_id=1, source_target_pairs={{0,2},{2,4},{4,6},{6,8},{8,10},{10,12},{12,14},{14,16},{16,18},{18... | collective-permute-start | bytes 940040 | tf_op jit(solution)/shard_map/ppermute | solution.py:23
  127.4 12.9 %collective-permute-start.2 = (f32[1,34,18,128]{3,1,2,0:T(8,128)S(1)}, f32[1,34,18,128]{3,1,2,0:T(8,128)S(1)}, u32[]{:S(2)}, u32[]{:S(2)}) collective-permute-start(f32[1,34,18,128]{3,1,2,0:T(8,128)S(1)} %fusion.31), channel_id=1, source_target_pairs={{2,0},{4,2},{6,4},{8,6},{10,8},{12,10},{14,12},{16,14},{18,16},{20... | collective-permute-start | bytes 940040 | tf_op jit(solution)/shard_map/ppermute | solution.py:25
  191.5 13.1 %collective-permute-start.5 = (f32[1,34,18,128]{3,1,2,0:T(8,128)S(1)}, f32[1,34,18,128]{3,1,2,0:T(8,128)S(1)}, u32[]{:S(2)}, u32[]{:S(2)}) collective-permute-start(f32[1,34,18,128]{3,1,2,0:T(8,128)S(1)} %fusion.32), channel_id=1, source_target_pairs={{0,2},{2,4},{4,6},{6,8},{8,10},{10,12},{12,14},{14,16},{16,18},{18... | collective-permute-start | bytes 940040 | tf_op jit(solution)/shard_map/ppermute | solution.py:23
  193.5 12.9 %collective-permute-start.4 = (f32[1,34,18,128]{3,1,2,0:T(8,128)S(1)}, f32[1,34,18,128]{3,1,2,0:T(8,128)S(1)}, u32[]{:S(2)}, u32[]{:S(2)}) collective-permute-start(f32[1,34,18,128]{3,1,2,0:T(8,128)S(1)} %fusion.32), channel_id=1, source_target_pairs={{2,0},{4,2},{6,4},{8,6},{10,8},{12,10},{14,12},{16,14},{18,16},{20... | collective-permute-start | bytes 940040 | tf_op jit(solution)/shard_map/ppermute | solution.py:25
where the time goes:
time: 216 us; the launch traced here: 213 us
  matrix products  87.2 us (40%)
  local copies, waits for them, and re-layouts  50.4 us (23%)
  starting transfers between devices  30.2 us (14%)
  blocking collectives  22.4 us (10%)
  waiting for transfers between devices  14.9 us (7%)
  other arithmetic  4.5 us (2%)
    dot_general x54, matrix products, add_block(): jnp.einsum('tib,iab->tia', piece, block, preferred_element_type=jnp.float32)  82 us
    gather x54, local copies, waits for them, and re-layouts, add_block(): piece = jnp.take(flexibility_tiles, column_slice, axis=1)  31 us
    ppermute x3, starting transfers between devices, with_halo(): lax.ppermute(head, axis, [((i + 1) % count, i) for i in range(ends)])  24.5 us
    all_gather x3, blocking collectives, shards(): lax.all_gather(robin_sum.astype(jnp.bfloat16), 'row', axis=1, tiled=True)  22.4 us
    unnamed x26, local copies, waits for them, and re-layouts  9.97 us
    ppermute x3, waiting for transfers between devices, with_halo(): lax.ppermute(tail, axis, [(i, (i + 1) % count) for i in range(ends)])  9.67 us
    ppermute x3, starting transfers between devices, with_halo(): lax.ppermute(tail, axis, [(i, (i + 1) % count) for i in range(ends)])  5.76 us
    ppermute x3, waiting for transfers between devices, with_halo(): lax.ppermute(head, axis, [((i + 1) % count, i) for i in range(ends)])  5.22 us
  transfers between devices with their start and end apart: 6, of which 6 were waited for; matrix products, arithmetic and copies ran while one was open for 0% of the time, Pallas kernels for 0%

commit v1 on v0

v1 whole, which is shorter than its diff:
```python
import functools

import jax
import jax.numpy as jnp
from jax import lax
from jax.experimental import pallas as pl
from jax.experimental.pallas import tpu as pltpu
from jax.sharding import PartitionSpec as P

EXTENT = 128
ITERS = 3
ONSET = 0.15
FAILURE = 1.5
MESH = pl.DeviceIdType.MESH


def running_max(values):
    times = values.shape[0]
    step = 1
    while step < times:
        fill = jnp.zeros((step, values.shape[1]), values.dtype)
        values = jnp.maximum(values, jnp.concatenate([fill, values[: times - step]], axis=0))
        step *= 2
    return values


def kernel(
    columns,
    partners,
    compliance_hbm,
    load_hbm,
    motion_hbm,
    traction_hbm,
    stiffness,
    history,
    orientation,
    motion_out,
    traction_out,
    *scratch,
):
    (compliance, load, motion, traction, robin, own_law, law_below, law_above, pair_law) = scratch[:9]
    halves = scratch[9:12]
    ascents = scratch[12:15]
    belows = scratch[15:18]
    aboves = scratch[18:21]
    (block_sem, input_sem, law_send, law_recv, row_send, row_recv, up_send, down_send, below_recv, above_recv) = scratch[21:]

    faces = compliance.shape[0]
    stored = compliance.shape[1]
    times = motion.shape[0]
    group = faces // 2
    sub = lax.axis_index("sub")
    row = lax.axis_index("row")
    last = lax.axis_size("sub") - 1
    has_below = sub > 0
    has_above = sub < last
    below = jnp.maximum(sub - 1, 0)
    above = jnp.minimum(sub + 1, last)

    def lanes(face):
        if isinstance(face, int):
            return pl.ds(face * EXTENT, EXTENT)
        return pl.ds(pl.multiple_of(face * EXTENT, EXTENT), EXTENT)

    motion_copy = pltpu.make_async_copy(motion_hbm, motion, input_sem.at[0])
    traction_copy = pltpu.make_async_copy(traction_hbm, traction, input_sem.at[1])
    load_copy = pltpu.make_async_copy(load_hbm, load, input_sem.at[2])
    motion_copy.start()
    traction_copy.start()

    barrier = pltpu.get_barrier_semaphore()
    pl.semaphore_signal(barrier, inc=1, device_id={"row": 1 - row}, device_id_type=MESH)

    @pl.when(has_below)
    def _():
        pl.semaphore_signal(barrier, inc=1, device_id={"sub": below}, device_id_type=MESH)

    @pl.when(has_above)
    def _():
        pl.semaphore_signal(barrier, inc=1, device_id={"sub": above}, device_id_type=MESH)

    def block_copy(face):
        return pltpu.make_async_copy(compliance_hbm.at[face], compliance.at[face], block_sem.at[face])

    for face in range(faces):
        block_copy(face).start()
    load_copy.start()

    for face in range(faces):
        own_law[face, 0:4] = jnp.broadcast_to(stiffness[0:1, lanes(face)], (4, EXTENT))
        own_law[face, 4:8] = jnp.broadcast_to(history[0:1, lanes(face)], (4, EXTENT))

    base = row * faces

    def send_half(iteration, face):
        return pltpu.make_async_remote_copy(
            src_ref=halves[iteration].at[base + face],
            dst_ref=halves[iteration].at[base + face],
            send_sem=row_send.at[iteration],
            recv_sem=row_recv.at[iteration],
            device_id={"row": 1 - row},
            device_id_type=MESH,
        )

    def all_halves(iteration):
        return pltpu.make_async_remote_copy(
            src_ref=halves[iteration].at[pl.ds(base, faces)],
            dst_ref=halves[iteration].at[pl.ds(base, faces)],
            send_sem=row_send.at[iteration],
            recv_sem=row_recv.at[iteration],
            device_id={"row": 1 - row},
            device_id_type=MESH,
        )

    motion_copy.wait()
    traction_copy.wait()
    for face in range(faces):
        total = traction[:, lanes(face)].astype(jnp.float32) + motion[:, lanes(face)].astype(jnp.float32)
        robin[face] = total
        halves[0][base + face] = total.astype(jnp.bfloat16)

    pl.semaphore_wait(barrier, 1 + has_below.astype(jnp.int32) + has_above.astype(jnp.int32))

    all_halves(0).start()

    def law_up():
        return pltpu.make_async_remote_copy(
            src_ref=own_law.at[pl.ds(0, group)],
            dst_ref=law_below,
            send_sem=law_send.at[0],
            recv_sem=law_recv.at[0],
            device_id={"sub": above},
            device_id_type=MESH,
        )

    def law_down():
        return pltpu.make_async_remote_copy(
            src_ref=own_law.at[pl.ds(group, group)],
            dst_ref=law_above,
            send_sem=law_send.at[1],
            recv_sem=law_recv.at[1],
            device_id={"sub": below},
            device_id_type=MESH,
        )

    def up(iteration, start, count):
        return pltpu.make_async_remote_copy(
            src_ref=ascents[iteration].at[pl.ds(start, count)],
            dst_ref=belows[iteration].at[pl.ds(start, count)],
            send_sem=up_send.at[iteration],
            recv_sem=below_recv.at[iteration],
            device_id={"sub": above},
            device_id_type=MESH,
        )

    def down(iteration, start, count):
        return pltpu.make_async_remote_copy(
            src_ref=ascents[iteration].at[pl.ds(group + start, count)],
            dst_ref=aboves[iteration].at[pl.ds(start, count)],
            send_sem=down_send.at[iteration],
            recv_sem=above_recv.at[iteration],
            device_id={"sub": below},
            device_id_type=MESH,
        )

    @pl.when(has_above)
    def _():
        law_up().start()

    @pl.when(has_below)
    def _():
        law_down().start()

    load_copy.wait()

    for iteration in range(ITERS):
        half = halves[iteration]
        ascent_buffer = ascents[iteration]
        all_halves(iteration).wait_recv()

        def linear(face):
            if iteration == 0:
                block_copy(face).wait()
            total = None
            for pair in range(stored // 2):
                left = half[columns[0, face, 2 * pair]]
                right = half[columns[0, face, 2 * pair + 1]]
                piece = jnp.concatenate([left, right], axis=1)
                block = jnp.concatenate([compliance[face, 2 * pair], compliance[face, 2 * pair + 1]], axis=1)
                product = lax.dot_general(
                    piece, block, (((1,), (1,)), ((), ())), preferred_element_type=jnp.float32
                )
                total = product if total is None else total + product
            response = load[:, lanes(face)].astype(jnp.float32) + total
            ascent_buffer[face] = robin[face] - 2.0 * response

        def linear_up(face, carry):
            linear(face)

            @pl.when(has_above)
            def _():
                up(iteration, face, 1).start()

            return carry

        def linear_down(face, carry):
            linear(group + face)

            @pl.when(has_below)
            def _():
                down(iteration, face, 1).start()

            return carry

        lax.fori_loop(0, group, linear_up, 0)
        lax.fori_loop(0, group, linear_down, 0)

        def local(face, mates, mate_laws):
            partner = partners[0, face]
            index = jnp.maximum(partner, 0)
            turn = orientation[pl.ds(face, 1)]
            if iteration == 0:
                mate_law = jnp.take_along_axis(
                    mate_laws[index], jnp.broadcast_to(turn, (8, EXTENT)), axis=1
                )
                law = own_law[face]
                rigidity = 0.5 * (law[0:4] + mate_law[0:4])
                record = jnp.maximum(law[4:8], mate_law[4:8])
                pair_law[face, 0:4] = rigidity
                pair_law[face, 4:8] = record
            else:
                law = pair_law[face]
                rigidity = law[0:4]
                record = law[4:8]
            rigidity = rigidity[0:1]
            record = record[0:1]
            mate = jnp.take_along_axis(mates[index], jnp.broadcast_to(turn, (times, EXTENT)), axis=1)
            ascent = ascent_buffer[face]
            difference = ascent - mate
            jump = difference * (1.0 / (1.0 + 2.0 * rigidity))
            peak = jnp.maximum(record, running_max(jnp.abs(jump)))
            damage = jnp.clip((peak - ONSET) * (1.0 / (FAILURE - ONSET)), 0.0, 1.0)
            effective = rigidity * (1.0 - damage)
            live = jnp.full((times, EXTENT), partner, jnp.int32) >= 0
            stress = jnp.where(live, effective * difference / (1.0 + 2.0 * effective), 0.0)
            shift = stress - ascent
            if iteration == ITERS - 1:
                motion_out[:, lanes(face)] = shift.astype(jnp.bfloat16)
                traction_out[:, lanes(face)] = stress.astype(jnp.bfloat16)
            else:
                total = stress + shift
                robin[face] = total
                halves[iteration + 1][base + face] = total.astype(jnp.bfloat16)
                send_half(iteration + 1, face).start()

        @pl.when(has_below)
        def _():
            if iteration == 0:
                law_up().wait_recv()
            up(iteration, 0, group).wait_recv()

        def local_down(face, carry):
            local(group + face, belows[iteration], law_below)
            return carry

        lax.fori_loop(0, group, local_down, 0)

        @pl.when(has_above)
        def _():
            if iteration == 0:
                law_down().wait_recv()
            down(iteration, 0, group).wait_recv()

        def local_up(face, carry):
            local(face, aboves[iteration], law_above)
            return carry

        lax.fori_loop(0, group, local_up, 0)

    for iteration in range(ITERS):
        all_halves(iteration).wait_send()

    @pl.when(has_above)
    def _():
        law_up().wait_send()
        for iteration in range(ITERS):
            up(iteration, 0, group).wait_send()

    @pl.when(has_below)
    def _():
        law_down().wait_send()
        for iteration in range(ITERS):
            down(iteration, 0, group).wait_send()


def shards(
    compliance,
    block_columns,
    load_response,
    starting_motion,
    start_traction,
    stiffness,
    history,
    face_partner,
    orientation,
):
    faces, stored = block_columns.shape[1:]
    times, width = starting_motion.shape[1:]
    group = faces // 2
    rows = lax.axis_size("row")
    smem = pl.BlockSpec(memory_space=pltpu.SMEM)
    vmem = pl.BlockSpec(memory_space=pltpu.VMEM)
    hbm = pl.BlockSpec(memory_space=pl.ANY)
    bf16 = jnp.bfloat16
    f32 = jnp.float32
    dma = pltpu.SemaphoreType.DMA
    scratch = (
        [
            pltpu.VMEM((faces, stored, EXTENT, EXTENT), bf16),
            pltpu.VMEM((times, width), bf16),
            pltpu.VMEM((times, width), bf16),
            pltpu.VMEM((times, width), bf16),
            pltpu.VMEM((faces, times, EXTENT), f32),
            pltpu.VMEM((faces, 8, EXTENT), f32),
            pltpu.VMEM((group, 8, EXTENT), f32),
            pltpu.VMEM((group, 8, EXTENT), f32),
            pltpu.VMEM((faces, 8, EXTENT), f32),
        ]
        + [pltpu.VMEM((rows * faces, times, EXTENT), bf16)] * ITERS
        + [pltpu.VMEM((faces, times, EXTENT), f32)] * ITERS
        + [pltpu.VMEM((group, times, EXTENT), f32)] * (2 * ITERS)
        + [dma((faces,)), dma((3,)), dma((2,)), dma((2,))]
        + [dma((ITERS,))] * 6
    )
    motion, traction = pl.pallas_call(
        kernel,
        out_shape=[jax.ShapeDtypeStruct((times, width), bf16)] * 2,
        in_specs=[smem, smem, hbm, hbm, hbm, hbm, vmem, vmem, vmem],
        out_specs=[vmem, vmem],
        scratch_shapes=scratch,
        compiler_params=pltpu.CompilerParams(
            collective_id=0, has_side_effects=True, vmem_limit_bytes=40 << 20
        ),
        name="latin",
    )(
        block_columns,
        face_partner,
        compliance[0],
        load_response[0],
        starting_motion[0],
        start_traction[0],
        stiffness,
        history,
        orientation[0],
    )
    return motion[None], traction[None]


def solution(mesh):
    in_specs = (
        P("sub", "row", None, None, None),
        P("sub", "row", None),
        P("sub", None, "row"),
        P("sub", None, "row"),
        P("sub", None, "row"),
        P("sub", "row"),
        P("sub", "row"),
        P("sub", "row"),
        P("sub", "row", None),
    )
    out_specs = (P("sub", None, "row"), P("sub", None, "row"))
    return jax.shard_map(shards, mesh=mesh, in_specs=in_specs, out_specs=out_specs, check_vma=False)
```

time: 216 us -> 64 us (0.30); the launches traced: 213 us -> 63.7 us
  matrix products: 87.2 us -> 0 us
  Pallas kernels: 0 us -> 51.5 us
  local copies, waits for them, and re-layouts: 50.4 us -> 11.5 us
  starting transfers between devices: 30.2 us -> 0 us
  blocking collectives: 22.4 us -> 0 us
  waiting for transfers between devices: 14.9 us -> 0 us
  other arithmetic: 4.5 us -> 0 us
    dot_general x57 -> x0, matrix products: 87.2 us -> none  [the longest x54 82 us: add_block(): jnp.einsum('tib,iab->tia', piece, block, preferred_element_type=jnp.float32)]
    pallas_call x0 -> x1, Pallas kernels: none -> 51.5 us  [shards(): pl.pallas_call(kernel, out_shape=[jax.ShapeDtypeStruct((times, width), bf...]
    gather x57 -> x0, local copies, waits for them, and re-layouts: 32.8 us -> none  [the longest x54 31 us: add_block(): piece = jnp.take(flexibility_tiles, column_slice, axis=1)]
    ppermute x6 -> x0, starting transfers between devices: 30.2 us -> none  [the longest x3 24.5 us: with_halo(): lax.ppermute(head, axis, [((i + 1) % count, i) for i in range(ends)])]
    all_gather x3 -> x0, blocking collectives: 22.4 us -> none  [shards(): lax.all_gather(robin_sum.astype(jnp.bfloat16), 'row', axis=1, tiled=True)]
    ppermute x6 -> x0, waiting for transfers between devices: 14.9 us -> none  [the longest x3 9.67 us: with_halo(): lax.ppermute(tail, axis, [(i, (i + 1) % count) for i in range(ends)])]
    pad x24 -> x0, local copies, waits for them, and re-layouts: 3.99 us -> none  [cohesive(): running_peak = lax.associative_scan(jnp.maximum, jnp.abs(jump_size), axis=0)]
    unnamed x26 -> x18, local copies, waits for them, and re-layouts: 9.97 us -> 11.5 us
  transfers between devices with their start and end apart: 6 -> 0, of which waited for: 6 -> 0; matrix products, arithmetic and copies ran while one was open for 0% -> 0% of each run, Pallas kernels for 0% -> 0%
where the time goes in v1:
time: 64 us; the launch traced here: 63.7 us
  Pallas kernels  51.5 us (80%)
  local copies, waits for them, and re-layouts  11.5 us (18%)
  between operations  0.65 us (1%)
    pallas_call x1, Pallas kernels, shards(): pl.pallas_call(kernel, out_shape=[jax.ShapeDtypeStruct((times, width), bf...  51.5 us
    unnamed x18, local copies, waits for them, and re-layouts  11.5 us

profile of v1, /device:TPU:2, one launch (start us, length us, event | category | flops | bytes accessed | tf_op | source)
XLA Modules:
  0.0 63.7 jit_solution(1731562227132691334)
XLA Ops:
  0.6 0.7 %copy.11.columns = s32[1,18,18]{2,1,0:T(8,128)S(1)} copy(s32[1,18,18]{2,0,1:T(1,128)} %param.10) | data formatting | bytes 2592 | tf_op args[1]
  1.3 0.7 %copy.14 = s32[1,18,128]{2,1,0:T(8,128)S(1)} copy(s32[1,18,128]{2,0,1:T(1,128)} %param.17) | data formatting | bytes 18432
  2.0 0.0 copy-start
  2.0 4.0 %copy-done = bf16[1,18,18,128,128]{4,3,2,1,0:T(8,128)(2,1)S(1)} copy-done((bf16[1,18,18,128,128]{4,3,2,1,0:T(8,128)(2,1)S(1)}, bf16[1,18,18,128,128]{4,3,2,1,0:T(8,128)(2,1)}, u32[]{:S(2)}) %copy-start) | copy-done | bytes 10616856
  6.0 0.0 copy-start.1
  6.1 0.9 %copy-done.1 = bf16[1,32,2304]{2,1,0:T(8,128)(2,1)S(1)} copy-done((bf16[1,32,2304]{2,1,0:T(8,128)(2,1)S(1)}, bf16[1,32,2304]{2,1,0:T(8,128)(2,1)}, u32[]{:S(2)}) %copy-start.1) | copy-done | bytes 147480
  7.0 0.0 copy-start.2
  7.0 0.9 %copy-done.2 = bf16[1,32,2304]{2,1,0:T(8,128)(2,1)S(1)} copy-done((bf16[1,32,2304]{2,1,0:T(8,128)(2,1)S(1)}, bf16[1,32,2304]{2,1,0:T(8,128)(2,1)}, u32[]{:S(2)}) %copy-start.2) | copy-done | bytes 147480
  7.9 0.0 copy-start.3
  7.9 0.9 %copy-done.3 = bf16[1,32,2304]{2,1,0:T(8,128)(2,1)S(1)} copy-done((bf16[1,32,2304]{2,1,0:T(8,128)(2,1)S(1)}, bf16[1,32,2304]{2,1,0:T(8,128)(2,1)}, u32[]{:S(2)}) %copy-start.3) | copy-done | bytes 147480
  8.8 0.0 copy-start.4
  8.8 0.7 %copy-done.4 = f32[1,2304]{1,0:T(1,128)S(1)} copy-done((f32[1,2304]{1,0:T(1,128)S(1)}, f32[1,2304]{1,0:T(1,128)}, u32[]{:S(2)}) %copy-start.4) | copy-done | bytes 9240
  9.5 0.0 copy-start.5
  9.5 0.7 %copy-done.5 = f32[1,2304]{1,0:T(1,128)S(1)} copy-done((f32[1,2304]{1,0:T(1,128)S(1)}, f32[1,2304]{1,0:T(1,128)}, u32[]{:S(2)}) %copy-start.5) | copy-done | bytes 9240
  10.2 0.0 copy-start.6
  10.2 0.7 %copy-done.6 = s32[1,18]{1,0:T(1,128)S(1)} copy-done((s32[1,18]{1,0:T(1,128)S(1)}, s32[1,18]{1,0:T(1,128)}, u32[]{:S(2)}) %copy-start.6) | copy-done | bytes 96
  10.8 51.5 %latin.1 = (bf16[32,2304]{1,0:T(8,128)(2,1)S(1)}, bf16[32,2304]{1,0:T(8,128)(2,1)S(1)}) custom-call(s32[1,18,18]{2,1,0:T(8,128)S(1)} %copy.11.columns, s32[1,18]{1,0:T(1,128)S(1)} %copy-done.6, bf16[18,18,128,128]{3,2,1,0:T(8,128)(2,1)S(1)} %bitcast.9, bf16[32,2304]{1,0:T(8,128)(2,1)S(1)} %bitcast.12, bf16[32,2304]{1,0:T(8,128)(2,1)S(1)} %bitcast.13, ...), custom_call_target="tpu_custom_call" | custom-call | tf_op jit(solution)/shard_map/latin/pallas_call | solution.py:335
  62.3 0.7 %copy.17 = bf16[1,32,2304]{2,1,0:T(8,128)(2,1)} copy(bf16[1,32,2304]{2,1,0:T(8,128)(2,1)S(1)} %bitcast.11) | data formatting | bytes 294912
  63.0 0.7 %copy.18 = bf16[1,32,2304]{2,1,0:T(8,128)(2,1)} copy(bf16[1,32,2304]{2,1,0:T(8,128)(2,1)S(1)} %bitcast.10) | data formatting | bytes 294912
Async XLA Ops:
  2.0 4.0 %copy-start = (bf16[1,18,18,128,128]{4,3,2,1,0:T(8,128)(2,1)S(1)}, bf16[1,18,18,128,128]{4,3,2,1,0:T(8,128)(2,1)}, u32[]{:S(2)}) copy-start(bf16[1,18,18,128,128]{4,3,2,1,0:T(8,128)(2,1)} %param.9) | copy-start | bytes 31850500
  6.0 0.9 %copy-start.1 = (bf16[1,32,2304]{2,1,0:T(8,128)(2,1)S(1)}, bf16[1,32,2304]{2,1,0:T(8,128)(2,1)}, u32[]{:S(2)}) copy-start(bf16[1,32,2304]{2,1,0:T(8,128)(2,1)} %param.11) | copy-start | bytes 442372
  7.0 0.9 %copy-start.2 = (bf16[1,32,2304]{2,1,0:T(8,128)(2,1)S(1)}, bf16[1,32,2304]{2,1,0:T(8,128)(2,1)}, u32[]{:S(2)}) copy-start(bf16[1,32,2304]{2,1,0:T(8,128)(2,1)} %param.12) | copy-start | bytes 442372
  7.9 0.9 %copy-start.3 = (bf16[1,32,2304]{2,1,0:T(8,128)(2,1)S(1)}, bf16[1,32,2304]{2,1,0:T(8,128)(2,1)}, u32[]{:S(2)}) copy-start(bf16[1,32,2304]{2,1,0:T(8,128)(2,1)} %param.13) | copy-start | bytes 442372
  8.8 0.7 %copy-start.4 = (f32[1,2304]{1,0:T(1,128)S(1)}, f32[1,2304]{1,0:T(1,128)}, u32[]{:S(2)}) copy-start(f32[1,2304]{1,0:T(1,128)} %stiffness.1) | copy-start | bytes 27652
  9.5 0.7 %copy-start.5 = (f32[1,2304]{1,0:T(1,128)S(1)}, f32[1,2304]{1,0:T(1,128)}, u32[]{:S(2)}) copy-start(f32[1,2304]{1,0:T(1,128)} %history.1) | copy-start | bytes 27652
  10.2 0.7 %copy-start.6 = (s32[1,18]{1,0:T(1,128)S(1)}, s32[1,18]{1,0:T(1,128)}, u32[]{:S(2)}) copy-start(s32[1,18]{1,0:T(1,128)} %partners.1) | copy-start | bytes 220

commit v2 on v1

--- a/solution.py
+++ b/solution.py
@@ -25,20 +25,22 @@
 
 
 def kernel(
-    columns,
-    partners,
+    columns_hbm,
+    partners_hbm,
     compliance_hbm,
     load_hbm,
     motion_hbm,
     traction_hbm,
-    stiffness,
-    history,
-    orientation,
+    stiffness_hbm,
+    history_hbm,
+    orientation_hbm,
     motion_out,
     traction_out,
     *scratch,
 ):
     (compliance, load, motion, traction, robin, own_law, law_below, law_above, pair_law) = scratch[:9]
+    columns, partners, stiffness, history, orientation = scratch[9:14]
+    scratch = scratch[5:]
     halves = scratch[9:12]
     ascents = scratch[12:15]
     belows = scratch[15:18]
@@ -65,8 +67,20 @@
     motion_copy = pltpu.make_async_copy(motion_hbm, motion, input_sem.at[0])
     traction_copy = pltpu.make_async_copy(traction_hbm, traction, input_sem.at[1])
     load_copy = pltpu.make_async_copy(load_hbm, load, input_sem.at[2])
+    law_copies = [
+        pltpu.make_async_copy(stiffness_hbm, stiffness, input_sem.at[3]),
+        pltpu.make_async_copy(history_hbm, history, input_sem.at[4]),
+    ]
+    columns_copy = pltpu.make_async_copy(columns_hbm, columns, input_sem.at[5])
+    match_copies = [
+        pltpu.make_async_copy(partners_hbm, partners, input_sem.at[6]),
+        pltpu.make_async_copy(orientation_hbm, orientation, input_sem.at[7]),
+    ]
     motion_copy.start()
     traction_copy.start()
+    for copy in law_copies:
+        copy.start()
+    columns_copy.start()
 
     barrier = pltpu.get_barrier_semaphore()
     pl.semaphore_signal(barrier, inc=1, device_id={"row": 1 - row}, device_id_type=MESH)
@@ -85,10 +99,8 @@
     for face in range(faces):
         block_copy(face).start()
     load_copy.start()
-
-    for face in range(faces):
-        own_law[face, 0:4] = jnp.broadcast_to(stiffness[0:1, lanes(face)], (4, EXTENT))
-        own_law[face, 4:8] = jnp.broadcast_to(history[0:1, lanes(face)], (4, EXTENT))
+    for copy in match_copies:
+        copy.start()
 
     base = row * faces
 
@@ -123,6 +135,12 @@
 
     all_halves(0).start()
 
+    for copy in law_copies:
+        copy.wait()
+    for face in range(faces):
+        own_law[face, 0:4] = jnp.broadcast_to(stiffness[0:1, lanes(face)], (4, EXTENT))
+        own_law[face, 4:8] = jnp.broadcast_to(history[0:1, lanes(face)], (4, EXTENT))
+
     def law_up():
         return pltpu.make_async_remote_copy(
             src_ref=own_law.at[pl.ds(0, group)],
@@ -172,6 +190,7 @@
         law_down().start()
 
     load_copy.wait()
+    columns_copy.wait()
 
     for iteration in range(ITERS):
         half = halves[iteration]
@@ -183,8 +202,8 @@
                 block_copy(face).wait()
             total = None
             for pair in range(stored // 2):
-                left = half[columns[0, face, 2 * pair]]
-                right = half[columns[0, face, 2 * pair + 1]]
+                left = half[columns[face, 0, 2 * pair]]
+                right = half[columns[face, 0, 2 * pair + 1]]
                 piece = jnp.concatenate([left, right], axis=1)
                 block = jnp.concatenate([compliance[face, 2 * pair], compliance[face, 2 * pair + 1]], axis=1)
                 product = lax.dot_general(
@@ -218,7 +237,7 @@
         def local(face, mates, mate_laws):
             partner = partners[0, face]
             index = jnp.maximum(partner, 0)
-            turn = orientation[pl.ds(face, 1)]
+            turn = orientation[face]
             if iteration == 0:
                 mate_law = jnp.take_along_axis(
                     mate_laws[index], jnp.broadcast_to(turn, (8, EXTENT)), axis=1
@@ -253,6 +272,10 @@
                 halves[iteration + 1][base + face] = total.astype(jnp.bfloat16)
                 send_half(iteration + 1, face).start()
 
+        if iteration == 0:
+            for copy in match_copies:
+                copy.wait()
+
         @pl.when(has_below)
         def _():
             if iteration == 0:
@@ -308,9 +331,8 @@
     times, width = starting_motion.shape[1:]
     group = faces // 2
     rows = lax.axis_size("row")
-    smem = pl.BlockSpec(memory_space=pltpu.SMEM)
     vmem = pl.BlockSpec(memory_space=pltpu.VMEM)
-    hbm = pl.BlockSpec(memory_space=pl.ANY)
+    hbm = pl.BlockSpec(memory_space=pltpu.HBM)
     bf16 = jnp.bfloat16
     f32 = jnp.float32
     dma = pltpu.SemaphoreType.DMA
@@ -325,25 +347,30 @@
             pltpu.VMEM((group, 8, EXTENT), f32),
             pltpu.VMEM((group, 8, EXTENT), f32),
             pltpu.VMEM((faces, 8, EXTENT), f32),
+            pltpu.SMEM((faces, 1, stored), jnp.int32),
+            pltpu.SMEM((1, faces), jnp.int32),
+            pltpu.VMEM((1, width), f32),
+            pltpu.VMEM((1, width), f32),
+            pltpu.VMEM((faces, 1, EXTENT), jnp.int32),
         ]
         + [pltpu.VMEM((rows * faces, times, EXTENT), bf16)] * ITERS
         + [pltpu.VMEM((faces, times, EXTENT), f32)] * ITERS
         + [pltpu.VMEM((group, times, EXTENT), f32)] * (2 * ITERS)
-        + [dma((faces,)), dma((3,)), dma((2,)), dma((2,))]
+        + [dma((faces,)), dma((8,)), dma((2,)), dma((2,))]
         + [dma((ITERS,))] * 6
     )
     motion, traction = pl.pallas_call(
         kernel,
         out_shape=[jax.ShapeDtypeStruct((times, width), bf16)] * 2,
-        in_specs=[smem, smem, hbm, hbm, hbm, hbm, vmem, vmem, vmem],
+        in_specs=[hbm] * 9,
         out_specs=[vmem, vmem],
         scratch_shapes=scratch,
         compiler_params=pltpu.CompilerParams(
-            collective_id=0, has_side_effects=True, vmem_limit_bytes=40 << 20
+            collective_id=0, has_side_effects=True, vmem_limit_bytes=67043328
         ),
         name="latin",
     )(
-        block_columns,
+        jnp.transpose(block_columns, (1, 0, 2)),
         face_partner,
         compliance[0],
         load_response[0],
@@ -351,7 +378,7 @@
         start_traction[0],
         stiffness,
         history,
-        orientation[0],
+        jnp.transpose(orientation, (1, 0, 2)),
     )
     return motion[None], traction[None]
 

time: 64 us -> 53.8 us (0.84)
  local copies, waits for them, and re-layouts: 11.5 us -> 3.16 us
  Pallas kernels: 51.5 us -> 49.9 us
    unnamed x18 -> x2, local copies, waits for them, and re-layouts: 11.5 us -> 3.16 us
    pallas_call x1, Pallas kernels: 51.5 us -> 49.9 us  [shards(): pl.pallas_call(kernel, out_shape=[jax.ShapeDtypeStruct((times, width), bf...]
where the time goes in v2:
time: 53.8 us; the launch traced here: 53.7 us
  Pallas kernels  49.9 us (93%)
  local copies, waits for them, and re-layouts  3.16 us (6%)
  between operations  0.64 us (1%)
    pallas_call x1, Pallas kernels, shards(): pl.pallas_call(kernel, out_shape=[jax.ShapeDtypeStruct((times, width), bf...  49.9 us
    unnamed x2, local copies, waits for them, and re-layouts  3.16 us

profile of v2, /device:TPU:2, one launch (start us, length us, event | category | flops | bytes accessed | tf_op | source)
XLA Modules:
  0.0 53.7 jit_solution(215169246531582916)
XLA Ops:
  0.6 49.9 %latin.1 = (bf16[32,2304]{1,0:T(8,128)(2,1)}, bf16[32,2304]{1,0:T(8,128)(2,1)}) custom-call(s32[18,1,18]{2,1,0:T(1,128)} %bitcast.14, s32[1,18]{1,0:T(1,128)} %partners_hbm.1, bf16[18,18,128,128]{3,2,1,0:T(8,128)(2,1)} %bitcast.8, bf16[32,2304]{1,0:T(8,128)(2,1)} %bitcast.11, bf16[32,2304]{1,0:T(8,128)(2,1)} %bitcast.12, bf16[32,2304]{1,0:T(8,128)(2,1)} %bitcast.13, ...), custom_call_target="tpu_custom_call" | custom-call | tf_op jit(solution)/shard_map/latin/pallas_call | solution.py:362
  50.5 1.6 %copy.13 = bf16[1,32,2304]{2,1,0:T(8,128)(2,1)} copy(bf16[1,32,2304]{2,1,0:T(8,128)(2,1)} %bitcast.10) | data formatting | bytes 294912
  52.1 1.6 %copy.14 = bf16[1,32,2304]{2,1,0:T(8,128)(2,1)} copy(bf16[1,32,2304]{2,1,0:T(8,128)(2,1)} %bitcast.9) | data formatting | bytes 294912

commit v3 on v0

v3 whole, which is shorter than its diff:
```python
import jax
import jax.numpy as jnp
from jax import lax
from jax.experimental import pallas as pl
from jax.experimental.pallas import tpu as pltpu
from jax.sharding import PartitionSpec as P

EXTENT = 128
ITERS = 3
ONSET = 0.15
FAILURE = 1.5
SPAN = 1.0 / (FAILURE - ONSET)
CHUNK = 3
MESH = pl.DeviceIdType.MESH


def running_max(values):
    times = values.shape[0]
    step = 1
    while step < times:
        fill = jnp.zeros((step, values.shape[1]), values.dtype)
        values = jnp.maximum(values, jnp.concatenate([fill, values[: times - step]], axis=0))
        step *= 2
    return values


def kernel(
    columns_hbm,
    partners_hbm,
    compliance_hbm,
    load_hbm,
    motion_hbm,
    traction_hbm,
    stiffness_hbm,
    history_hbm,
    orientation_hbm,
    ascent_out,
    traction_out,
    compliance,
    load,
    motion,
    traction,
    columns,
    partners,
    stiffness,
    history,
    orientation,
    offset,
    own_law,
    near_law,
    far_law,
    pair_law,
    *scratch,
):
    halves = scratch[0:3]
    ascents = scratch[3:6]
    nears = scratch[6:9]
    fars = scratch[9:12]
    (block_sem, input_sem, law_send, law_recv, row_send, row_recv, near_send, near_recv, far_send, far_recv) = scratch[12:]

    faces, stored = compliance.shape[:2]
    times = motion.shape[0]
    group = faces // 2
    subs = lax.axis_size("sub")
    sub = lax.axis_index("sub")
    row = lax.axis_index("row")
    odd = lax.rem(sub, 2)
    near = {"sub": sub + 1 - 2 * odd}
    far = {"sub": lax.rem(sub + 2 * odd - 1 + subs, subs)}
    mirror = {"row": 1 - row}
    near_base = group * odd
    far_base = group * (1 - odd)
    base = row * faces

    def lanes(face):
        if isinstance(face, int):
            return pl.ds(face * EXTENT, EXTENT)
        return pl.ds(pl.multiple_of(face * EXTENT, EXTENT), EXTENT)

    def fetch(source, target, index):
        return pltpu.make_async_copy(source, target, input_sem.at[index])

    def block_copy(face):
        return pltpu.make_async_copy(compliance_hbm.at[face], compliance.at[face], block_sem.at[face])

    def push(source, target, send, recv, device):
        return pltpu.make_async_remote_copy(
            src_ref=source, dst_ref=target, send_sem=send, recv_sem=recv, device_id=device, device_id_type=MESH
        )

    motion_copy = fetch(motion_hbm, motion, 0)
    traction_copy = fetch(traction_hbm, traction, 1)
    stiffness_copy = fetch(stiffness_hbm, stiffness, 2)
    history_copy = fetch(history_hbm, history, 3)
    load_copy = fetch(load_hbm, load, 4)
    columns_copy = fetch(columns_hbm, columns, 5)
    partners_copy = fetch(partners_hbm, partners, 6)
    orientation_copy = fetch(orientation_hbm, orientation, 7)
    motion_copy.start()
    traction_copy.start()

    barrier = pltpu.get_barrier_semaphore()
    for device in (mirror, near, far):
        pl.semaphore_signal(barrier, inc=1, device_id=device, device_id_type=MESH)

    stiffness_copy.start()
    history_copy.start()
    load_copy.start()
    for face in range(faces):
        block_copy(face).start()
    for copy in (columns_copy, partners_copy, orientation_copy):
        copy.start()

    def send_half(iteration, start, count):
        part = halves[iteration].at[pl.ds(base + start, count)]
        return push(part, part, row_send.at[iteration], row_recv.at[iteration], mirror)

    def send_near(iteration, start, count):
        return push(
            ascents[iteration].at[pl.ds(near_base + start, count)],
            nears[iteration].at[pl.ds(start, count)],
            near_send.at[iteration],
            near_recv.at[iteration],
            near,
        )

    def send_far(iteration, start, count):
        return push(
            ascents[iteration].at[pl.ds(far_base + start, count)],
            fars[iteration].at[pl.ds(start, count)],
            far_send.at[iteration],
            far_recv.at[iteration],
            far,
        )

    near_law_copy = push(own_law.at[pl.ds(near_base, group)], near_law, law_send.at[0], law_recv.at[0], near)
    far_law_copy = push(own_law.at[pl.ds(far_base, group)], far_law, law_send.at[1], law_recv.at[1], far)

    motion_copy.wait()
    traction_copy.wait()
    for face in range(faces):
        total = traction[:, lanes(face)].astype(jnp.float32) + motion[:, lanes(face)].astype(jnp.float32)
        offset[face] = total
        halves[0][base + face] = total.astype(jnp.bfloat16)

    pl.semaphore_wait(barrier, 3)
    send_half(0, 0, faces).start()

    stiffness_copy.wait()
    history_copy.wait()
    for face in range(faces):
        own_law[face, 0:4] = jnp.broadcast_to(stiffness[0:1, lanes(face)], (4, EXTENT))
        own_law[face, 4:8] = jnp.broadcast_to(history[0:1, lanes(face)], (4, EXTENT))
    far_law_copy.start()
    near_law_copy.start()

    load_copy.wait()
    for face in range(faces):
        offset[face] = offset[face] - 2.0 * load[:, lanes(face)].astype(jnp.float32)

    def turn_blocks(face, carry):
        block_copy(face).wait()
        for slot in range(stored):
            compliance[face, slot] = compliance[face, slot].T
        return carry

    lax.fori_loop(0, faces, turn_blocks, 0)

    for copy in (columns_copy, partners_copy, orientation_copy):
        copy.wait()
    near_law_copy.wait_recv()
    far_law_copy.wait_recv()

    def join_laws(face, mate_laws):
        partner = partners[0, face]
        turn = jnp.broadcast_to(orientation[face], (8, EXTENT))
        mate = jnp.take_along_axis(mate_laws[jnp.maximum(partner, 0)], turn, axis=1)
        own = own_law[face]
        live = jnp.full((1, EXTENT), partner, jnp.int32) >= 0
        rigidity = jnp.where(live, 0.5 * (own[0:1] + mate[0:1]), 0.0)
        record = SPAN * jnp.maximum(own[4:5], mate[4:5])
        scale = SPAN / (1.0 + 2.0 * rigidity)
        pair_law[face, 0] = jnp.broadcast_to(rigidity, (8, EXTENT))
        pair_law[face, 1] = jnp.broadcast_to(record, (8, EXTENT))
        pair_law[face, 2] = jnp.broadcast_to(scale, (8, EXTENT))

    for index in range(group):
        join_laws(near_base + index, near_law)
    for index in range(group):
        join_laws(far_base + index, far_law)

    def tall(tile):
        return jnp.concatenate([tile] * (times // 8), axis=0)

    for iteration in range(ITERS):
        half = halves[iteration]
        ascent_buffer = ascents[iteration]
        send_half(iteration, 0, faces).wait_recv()

        def linear(face):
            total = None
            for pair in range(stored // 2):
                left = half[columns[face, 0, 2 * pair]]
                right = half[columns[face, 0, 2 * pair + 1]]
                piece = jnp.concatenate([left, right], axis=1)
                block = jnp.concatenate([compliance[face, 2 * pair], compliance[face, 2 * pair + 1]], axis=0)
                product = jnp.dot(piece, block, preferred_element_type=jnp.float32)
                total = product if total is None else total + product
            ascent_buffer[face] = offset[face] - 2.0 * total

        for start in range(0, group, CHUNK):
            for index in range(start, start + CHUNK):
                linear(far_base + index)
            send_far(iteration, start, CHUNK).start()
        for index in range(group):
            linear(near_base + index)
        send_near(iteration, 0, group).start()

        def local(face, mates):
            index = jnp.maximum(partners[0, face], 0)
            turn = jnp.broadcast_to(orientation[face], (times, EXTENT))
            rigidity = tall(pair_law[face, 0])
            record = tall(pair_law[face, 1])
            scale = tall(pair_law[face, 2])
            mate = jnp.take_along_axis(mates[index], turn, axis=1)
            ascent = ascent_buffer[face]
            difference = ascent - mate
            peak = jnp.maximum(record, running_max(jnp.abs(difference * scale)))
            effective = rigidity * jnp.clip(FAILURE * SPAN - peak, 0.0, 1.0)
            stress = effective * difference / (1.0 + 2.0 * effective)
            if iteration == ITERS - 1:
                ascent_out[:, lanes(face)] = ascent
                traction_out[:, lanes(face)] = stress
            else:
                total = stress + (stress - ascent)
                offset[face] = total - 2.0 * load[:, lanes(face)].astype(jnp.float32)
                halves[iteration + 1][base + face] = total.astype(jnp.bfloat16)

        send_near(iteration, 0, group).wait_recv()
        for start in range(0, group, CHUNK):
            for index in range(start, start + CHUNK):
                local(near_base + index, nears[iteration])
            if iteration < ITERS - 1:
                send_half(iteration + 1, near_base + start, CHUNK).start()
        send_far(iteration, 0, group).wait_recv()
        for start in range(0, group, CHUNK):
            for index in range(start, start + CHUNK):
                local(far_base + index, fars[iteration])
            if iteration < ITERS - 1:
                send_half(iteration + 1, far_base + start, CHUNK).start()

    near_law_copy.wait_send()
    far_law_copy.wait_send()
    for iteration in range(ITERS):
        send_half(iteration, 0, faces).wait_send()
        send_near(iteration, 0, group).wait_send()
        send_far(iteration, 0, group).wait_send()


def shards(
    compliance,
    block_columns,
    load_response,
    starting_motion,
    start_traction,
    stiffness,
    history,
    face_partner,
    orientation,
):
    faces, stored = block_columns.shape[1:]
    times, width = starting_motion.shape[1:]
    group = faces // 2
    rows = lax.axis_size("row")
    vmem = pl.BlockSpec(memory_space=pltpu.VMEM)
    hbm = pl.BlockSpec(memory_space=pltpu.HBM)
    bf16 = jnp.bfloat16
    f32 = jnp.float32
    dma = pltpu.SemaphoreType.DMA
    scratch = (
        [
            pltpu.VMEM((faces, stored, EXTENT, EXTENT), bf16),
            pltpu.VMEM((times, width), bf16),
            pltpu.VMEM((times, width), bf16),
            pltpu.VMEM((times, width), bf16),
            pltpu.SMEM((faces, 1, stored), jnp.int32),
            pltpu.SMEM((1, faces), jnp.int32),
            pltpu.VMEM((1, width), f32),
            pltpu.VMEM((1, width), f32),
            pltpu.VMEM((faces, 1, EXTENT), jnp.int32),
            pltpu.VMEM((faces, times, EXTENT), f32),
            pltpu.VMEM((faces, 8, EXTENT), f32),
            pltpu.VMEM((group, 8, EXTENT), f32),
            pltpu.VMEM((group, 8, EXTENT), f32),
            pltpu.VMEM((faces, 3, 8, EXTENT), f32),
        ]
        + [pltpu.VMEM((rows * faces, times, EXTENT), bf16)] * ITERS
        + [pltpu.VMEM((faces, times, EXTENT), f32)] * ITERS
        + [pltpu.VMEM((group, times, EXTENT), f32)] * (2 * ITERS)
        + [dma((faces,)), dma((8,)), dma((2,)), dma((2,))]
        + [dma((ITERS,))] * 6
    )
    ascent, traction = pl.pallas_call(
        kernel,
        out_shape=[jax.ShapeDtypeStruct((times, width), f32)] * 2,
        in_specs=[hbm] * 9,
        out_specs=[vmem, vmem],
        scratch_shapes=scratch,
        compiler_params=pltpu.CompilerParams(
            collective_id=0, has_side_effects=True, vmem_limit_bytes=67043328
        ),
        name="latin",
    )(
        jnp.transpose(block_columns, (1, 0, 2)),
        face_partner,
        compliance[0],
        load_response[0],
        starting_motion[0],
        start_traction[0],
        stiffness,
        history,
        jnp.transpose(orientation, (1, 0, 2)),
    )
    return (traction - ascent).astype(bf16)[None], traction.astype(bf16)[None]


def solution(mesh):
    in_specs = (
        P("sub", "row", None, None, None),
        P("sub", "row", None),
        P("sub", None, "row"),
        P("sub", None, "row"),
        P("sub", None, "row"),
        P("sub", "row"),
        P("sub", "row"),
        P("sub", "row"),
        P("sub", "row", None),
    )
    out_specs = (P("sub", None, "row"), P("sub", None, "row"))
    return jax.shard_map(shards, mesh=mesh, in_specs=in_specs, out_specs=out_specs, check_vma=False)
```

time: 216 us -> 44.5 us (0.21)
  the two profiles are of different devices: /device:TPU:2 before, /device:TPU:4 now
where the time goes in v3:
time: 44.5 us; the launch traced here: 44.4 us
  Pallas kernels  41.9 us (94%)
  other arithmetic  1.89 us (4%)
  between operations  0.64 us (1%)
    pallas_call x1, Pallas kernels, shards(): pl.pallas_call(kernel, out_shape=[jax.ShapeDtypeStruct((times, width), f3...  41.9 us
    broadcast_in_dim x1, other arithmetic, shards(): return ((traction - ascent).astype(bf16)[None], traction.astype(bf16)[None])  1.89 us

profile of v3, /device:TPU:4, one launch (start us, length us, event | category | flops | bytes accessed | tf_op | source)
XLA Modules:
  0.0 44.4 jit_solution(18289432831720946877)
XLA Ops:
  0.6 41.9 %latin.1 = (f32[32,2304]{1,0:T(8,128)}, f32[32,2304]{1,0:T(8,128)}) custom-call(s32[18,1,18]{2,1,0:T(1,128)} %bitcast.14, s32[1,18]{1,0:T(1,128)} %partners_hbm.1, bf16[18,18,128,128]{3,2,1,0:T(8,128)(2,1)} %bitcast.10, bf16[32,2304]{1,0:T(8,128)(2,1)} %bitcast.11, bf16[32,2304]{1,0:T(8,128)(2,1)} %bitcast.12, bf16[32,2304]{1,0:T(8,128)(2,1)} %bitcast.13, ...), custom_call_target="tpu_custom_call" | custom-call | tf_op jit(solution)/shard_map/latin/pallas_call | solution.py:303
  42.5 1.9 %convert_bitcast_fusion = (bf16[1,32,2304]{2,1,0:T(8,128)(2,1)}, bf16[1,32,2304]{2,1,0:T(8,128)(2,1)}) fusion(f32[32,2304]{1,0:T(8,128)} %get-tuple-element.4, f32[32,2304]{1,0:T(8,128)} %get-tuple-element.5), kind=kLoop, calls=%fused_computation.2 | loop fusion | flops 221184 | bytes 884736 | tf_op jit(solution)/shard_map/broadcast_in_dim | solution.py:324

commit v4 on v3

--- a/solution.py
+++ b/solution.py
@@ -300,6 +300,9 @@
         + [dma((faces,)), dma((8,)), dma((2,)), dma((2,))]
         + [dma((ITERS,))] * 6
     )
+    def keep(array):
+        return pltpu.with_memory_space_constraint(array, pltpu.HBM)
+
     ascent, traction = pl.pallas_call(
         kernel,
         out_shape=[jax.ShapeDtypeStruct((times, width), f32)] * 2,
@@ -307,19 +310,19 @@
         out_specs=[vmem, vmem],
         scratch_shapes=scratch,
         compiler_params=pltpu.CompilerParams(
-            collective_id=0, has_side_effects=True, vmem_limit_bytes=67043328
+            collective_id=0, has_side_effects=True, vmem_limit_bytes=20 << 20
         ),
         name="latin",
     )(
-        jnp.transpose(block_columns, (1, 0, 2)),
-        face_partner,
-        compliance[0],
-        load_response[0],
-        starting_motion[0],
-        start_traction[0],
-        stiffness,
-        history,
-        jnp.transpose(orientation, (1, 0, 2)),
+        keep(jnp.transpose(block_columns, (1, 0, 2))),
+        keep(face_partner),
+        keep(compliance[0]),
+        keep(load_response[0]),
+        keep(starting_motion[0]),
+        keep(start_traction[0]),
+        keep(stiffness),
+        keep(history),
+        keep(jnp.transpose(orientation, (1, 0, 2))),
     )
     return (traction - ascent).astype(bf16)[None], traction.astype(bf16)[None]
 

time: 44.5 us -> 42.5 us (0.955)
  the two profiles are of different devices: /device:TPU:4 before, /device:TPU:1 now
where the time goes in v4:
time: 42.5 us
  Pallas kernels  41.1 us (97%)
  other arithmetic  0.74 us (2%)
  between operations  0.64 us (2%)
    pallas_call x1, Pallas kernels, shards(): pl.pallas_call(kernel, out_shape=[jax.ShapeDtypeStruct((times, width), f3...  41.1 us

profile of v4, /device:TPU:1, one launch (start us, length us, event | category | flops | bytes accessed | tf_op | source)
XLA Modules:
  0.0 42.5 jit_solution(13745843062398489470)
XLA Ops:
  0.6 41.1 %latin.1 = (f32[32,2304]{1,0:T(8,128)S(1)}, f32[32,2304]{1,0:T(8,128)S(1)}) custom-call(s32[18,1,18]{2,1,0:T(1,128)} %bitcast.14, s32[1,18]{1,0:T(1,128)} %partners_hbm.1, bf16[18,18,128,128]{3,2,1,0:T(8,128)(2,1)} %bitcast.10, bf16[32,2304]{1,0:T(8,128)(2,1)} %bitcast.11, bf16[32,2304]{1,0:T(8,128)(2,1)} %bitcast.12, bf16[32,2304]{1,0:T(8,128)(2,1)} %bitcast.13, ...), custom_call_target="tpu_custom_call" | custom-call | tf_op jit(solution)/shard_map/latin/pallas_call | solution.py:306
  41.7 0.7 %convert_bitcast_fusion = (bf16[1,32,2304]{2,1,0:T(8,128)(2,1)}, bf16[1,32,2304]{2,1,0:T(8,128)(2,1)}) fusion(f32[32,2304]{1,0:T(8,128)S(1)} %get-tuple-element.4, f32[32,2304]{1,0:T(8,128)S(1)} %get-tuple-element.5), kind=kLoop, calls=%fused_computation.2 | loop fusion | flops 221184 | bytes 884736 | tf_op jit(solution)/shard_map/broadcast_in_dim | solution.py:327

commit v5 on v4

--- a/solution.py
+++ b/solution.py
@@ -11,6 +11,7 @@
 FAILURE = 1.5
 SPAN = 1.0 / (FAILURE - ONSET)
 CHUNK = 3
+COLUMN = 16
 MESH = pl.DeviceIdType.MESH
 
 
@@ -66,7 +67,8 @@
     row = lax.axis_index("row")
     odd = lax.rem(sub, 2)
     near = {"sub": sub + 1 - 2 * odd}
-    far = {"sub": lax.rem(sub + 2 * odd - 1 + subs, subs)}
+    end = jnp.logical_or(sub == 0, sub == subs - 1)
+    far = {"sub": jnp.where(end, sub, sub + 2 * odd - 1), "row": jnp.where(end, 1 - row, row)}
     mirror = {"row": 1 - row}
     near_base = group * odd
     far_base = group * (1 - odd)
@@ -99,9 +101,21 @@
     motion_copy.start()
     traction_copy.start()
 
+    place = lax.rem(sub, COLUMN)
+    inner = jnp.logical_not(end)
+    leads = jnp.logical_and(inner, place == 0)
+    answers = jnp.logical_and(inner, place == COLUMN - 1)
+
+    def greet(device):
+        pl.semaphore_signal(barrier, inc=1, device_id=device, device_id_type=MESH)
+
     barrier = pltpu.get_barrier_semaphore()
-    for device in (mirror, near, far):
-        pl.semaphore_signal(barrier, inc=1, device_id=device, device_id_type=MESH)
+    greet(mirror)
+    greet(near)
+
+    @pl.when(jnp.logical_not(jnp.logical_or(leads, answers)))
+    def _():
+        greet(far)
 
     stiffness_copy.start()
     history_copy.start()
@@ -143,16 +157,23 @@
         offset[face] = total
         halves[0][base + face] = total.astype(jnp.bfloat16)
 
-    pl.semaphore_wait(barrier, 3)
+    pl.semaphore_wait(barrier, 3 - leads.astype(jnp.int32))
     send_half(0, 0, faces).start()
+
+    @pl.when(jnp.logical_or(leads, answers))
+    def _():
+        greet(far)
 
     stiffness_copy.wait()
     history_copy.wait()
     for face in range(faces):
         own_law[face, 0:4] = jnp.broadcast_to(stiffness[0:1, lanes(face)], (4, EXTENT))
         own_law[face, 4:8] = jnp.broadcast_to(history[0:1, lanes(face)], (4, EXTENT))
-    far_law_copy.start()
     near_law_copy.start()
+
+    @pl.when(jnp.logical_not(leads))
+    def _():
+        far_law_copy.start()
 
     load_copy.wait()
     for face in range(faces):
@@ -169,7 +190,6 @@
     for copy in (columns_copy, partners_copy, orientation_copy):
         copy.wait()
     near_law_copy.wait_recv()
-    far_law_copy.wait_recv()
 
     def join_laws(face, mate_laws):
         partner = partners[0, face]
@@ -186,8 +206,6 @@
 
     for index in range(group):
         join_laws(near_base + index, near_law)
-    for index in range(group):
-        join_laws(far_base + index, far_law)
 
     def tall(tile):
         return jnp.concatenate([tile] * (times // 8), axis=0)
@@ -211,6 +229,13 @@
         for start in range(0, group, CHUNK):
             for index in range(start, start + CHUNK):
                 linear(far_base + index)
+            if iteration == 0 and start == 0:
+
+                @pl.when(leads)
+                def _():
+                    pl.semaphore_wait(barrier, 1)
+                    far_law_copy.start()
+
             send_far(iteration, start, CHUNK).start()
         for index in range(group):
             linear(near_base + index)
@@ -242,6 +267,10 @@
                 local(near_base + index, nears[iteration])
             if iteration < ITERS - 1:
                 send_half(iteration + 1, near_base + start, CHUNK).start()
+        if iteration == 0:
+            far_law_copy.wait_recv()
+            for index in range(group):
+                join_laws(far_base + index, far_law)
         send_far(iteration, 0, group).wait_recv()
         for start in range(0, group, CHUNK):
             for index in range(start, start + CHUNK):

time: 42.5 us -> 41.5 us (0.976)
  the two profiles are of different devices: /device:TPU:1 before, /device:TPU:2 now
where the time goes in v5:
time: 41.5 us; the launch traced here: 41.4 us
  Pallas kernels  40 us (96%)
  other arithmetic  0.74 us (2%)
  between operations  0.64 us (2%)
    pallas_call x1, Pallas kernels, shards(): pl.pallas_call(kernel, out_shape=[jax.ShapeDtypeStruct((times, width), f3...  40 us

profile of v5, /device:TPU:2, one launch (start us, length us, event | category | flops | bytes accessed | tf_op | source)
XLA Modules:
  0.0 41.4 jit_solution(14140867093471274611)
XLA Ops:
  0.6 40.0 %latin.1 = (f32[32,2304]{1,0:T(8,128)S(1)}, f32[32,2304]{1,0:T(8,128)S(1)}) custom-call(s32[18,1,18]{2,1,0:T(1,128)} %bitcast.14, s32[1,18]{1,0:T(1,128)} %partners_hbm.1, bf16[18,18,128,128]{3,2,1,0:T(8,128)(2,1)} %bitcast.10, bf16[32,2304]{1,0:T(8,128)(2,1)} %bitcast.11, bf16[32,2304]{1,0:T(8,128)(2,1)} %bitcast.12, bf16[32,2304]{1,0:T(8,128)(2,1)} %bitcast.13, ...), custom_call_target="tpu_custom_call" | custom-call | tf_op jit(solution)/shard_map/latin/pallas_call | solution.py:335
  40.7 0.7 %convert_bitcast_fusion = (bf16[1,32,2304]{2,1,0:T(8,128)(2,1)}, bf16[1,32,2304]{2,1,0:T(8,128)(2,1)}) fusion(f32[32,2304]{1,0:T(8,128)S(1)} %get-tuple-element.4, f32[32,2304]{1,0:T(8,128)S(1)} %get-tuple-element.5), kind=kLoop, calls=%fused_computation.2 | loop fusion | flops 221184 | bytes 884736 | tf_op jit(solution)/shard_map/broadcast_in_dim | solution.py:356
